TPU v7x, 32 devices: a whole 2x2x4 slice. The times are simulated.
32 devices in a mesh: grp: 2 (over y), seq: 16 (over z, x, core).
Axes of the slice: x: 2, y: 2, z: 4, core: 2. Of those that a mesh axis runs over, the one named last changes fastest.
Arguments:
- inputs: bfloat16 [4, 2048, 1536], P('grp', 'seq'), parts along dimension 0, may hold values from -36 to 36
- gain: float32 [1536], replicated, may hold values from 0.1 to 1.9
- conv_weight: bfloat16 [3, 1536, 768], P(None, 'seq'), may hold values from -0.09375 to 0.09375
- proj_weight: bfloat16 [768, 1536], P(None, 'seq'), may hold values from -0.21875 to 0.21875
- head_weight: bfloat16 [1536, 512], P(None, 'seq'), may hold values from -0.15625 to 0.15625
- track_head_bias: bfloat16 [1, 512], P(None, 'seq'), may hold values from -4 to 4
- counts: int32 [4, 2048, 512], P('grp', 'seq'), parts along dimension 0, may hold values from 0 to 32
Outputs:
- input_grad: bfloat16 [4, 2048, 1536], P('grp', 'seq'), parts along dimension 0
- loss_value: float32 [2], P('grp'), parts along dimension 0
There are 2 independent parts, one for each index of `grp`. A program takes and returns all parts, laid end to end along the dimension named above; an argument that names none is the same for every part. Nothing has to cross between parts.
All inputs are finite; a program needn't handle non-finite values.
Results may differ from a plain program's by a relative error of at most 0.011.
Values may be sent and summed in bfloat16 or wider, within the bound.
A program may use at most 128 MiB of HBM per device.

v0:
```python
import jax
import jax.numpy as jnp
from jax import lax
from jax.sharding import PartitionSpec as P

SPAN = 8


def shifted(value, axis, steps):
    count = lax.axis_size(axis)
    initial, last = (max(0, -steps), min(count, count - steps))
    return lax.ppermute(value, axis, [(source, source + steps) for source in range(initial, last)])


def norm_rows(value_entries, gain):
    scale_inv = lax.rsqrt(jnp.mean(value_entries * value_entries, axis=-1, keepdims=True) + 1e-06)
    return value_entries * scale_inv * gain


def head_block(stream, head_full, bias_full, observed):
    logits = jnp.dot(stream, head_full, preferred_element_type=jnp.float32) + bias_full.astype(
        jnp.float32
    )
    poisson_rate = jax.nn.softplus(logits) + 0.05
    observed_f = observed.astype(jnp.float32)
    loss_total = jnp.sum(poisson_rate - observed_f * jnp.log(poisson_rate))
    logit_grad = ((1.0 - observed_f / poisson_rate) * jax.nn.sigmoid(logits)).astype(jnp.bfloat16)
    residual_gradient = lax.dot_general(
        logit_grad, head_full, (((1,), (1,)), ((), ())), preferred_element_type=jnp.float32
    )
    return (loss_total, residual_gradient)


def back_dot(left, right):
    return lax.dot_general(
        left, right, (((1,), (1,)), ((), ())), preferred_element_type=jnp.float32
    )


def shards(inputs, gain, conv_weight, proj_weight, head_weight, track_head_bias, counts):
    seq_count, row_count, window_width = inputs.shape
    flat_rows = seq_count * row_count
    track_count = counts.shape[2]
    conv_full, proj_full = (
        lax.all_gather(conv_weight, "seq", axis=1, tiled=True),
        lax.all_gather(proj_weight, "seq", axis=1, tiled=True),
    )
    inner = conv_full.shape[2]
    inputs_f = inputs.astype(jnp.float32)
    normed = norm_rows(inputs_f, gain).astype(jnp.bfloat16)
    normed_flat = normed.reshape(flat_rows, window_width)
    behind_rows = shifted(normed, "seq", SPAN).reshape(flat_rows, window_width)
    ahead_rows = shifted(normed, "seq", -SPAN).reshape(flat_rows, window_width)
    conv_pre = jnp.dot(normed_flat, conv_full[1], preferred_element_type=jnp.float32)
    conv_pre = conv_pre + jnp.dot(behind_rows, conv_full[0], preferred_element_type=jnp.float32)
    conv_pre = conv_pre + jnp.dot(ahead_rows, conv_full[2], preferred_element_type=jnp.float32)
    conv_act = jax.nn.gelu(conv_pre).astype(jnp.bfloat16)
    stream = (
        inputs_f.reshape(flat_rows, window_width)
        + jnp.dot(conv_act, proj_full, preferred_element_type=jnp.float32)
    ).astype(jnp.bfloat16)
    counts_flat = counts.reshape(flat_rows, track_count)
    head_full, bias_full = (
        lax.all_gather(head_weight, "seq", axis=1, tiled=True),
        lax.all_gather(track_head_bias, "seq", axis=1, tiled=True),
    )
    loss_total, residual_gradient = head_block(stream, head_full, bias_full, counts_flat)
    summed_loss = lax.psum(loss_total, "seq")
    loss_value = (summed_loss / (flat_rows * lax.axis_size("seq") * track_count)).reshape(1)
    act_grad = back_dot(residual_gradient.astype(jnp.bfloat16), proj_full)
    _, gelu_back = jax.vjp(jax.nn.gelu, conv_pre)
    pre_grad = gelu_back(act_grad)[0].astype(jnp.bfloat16)
    pre_three = pre_grad.reshape(seq_count, row_count, inner)
    grad_ahead = shifted(pre_three, "seq", -SPAN).reshape(flat_rows, inner)
    grad_behind = shifted(pre_three, "seq", SPAN).reshape(flat_rows, inner)
    normed_grad = back_dot(pre_grad, conv_full[1])
    normed_grad = normed_grad + back_dot(grad_ahead, conv_full[0])
    normed_grad = normed_grad + back_dot(grad_behind, conv_full[2])
    _, norm_back = jax.vjp(lambda value_entries: norm_rows(value_entries, gain), inputs_f)
    input_grad = (
        residual_gradient.reshape(seq_count, row_count, window_width)
        + norm_back(normed_grad.reshape(seq_count, row_count, window_width))[0]
    ).astype(jnp.bfloat16)
    return (input_grad, loss_value)


def solution(mesh):
    placed = (
        P("grp", "seq", None),
        P(),
        P(None, "seq", None),
        P(None, "seq"),
        P(None, "seq"),
        P(None, "seq"),
        P("grp", "seq", None),
    )
    return jax.shard_map(
        shards,
        mesh=mesh,
        in_specs=placed,
        out_specs=(P("grp", "seq", None), P("grp")),
        check_vma=False,
    )
```

profile of v0, /device:TPU:0, one launch (start us, length us, event | category | flops | bytes accessed | tf_op | source)
XLA Modules:
  0.0 252.3 jit_solution(4451681180811085461)
XLA Ops:
  7.2 0.7 all-gather.4.cloned.1.call-update
  8.0 0.7 all-gather.8.cloned.1.call-update
  8.7 0.7 all-gather.6.cloned.1.call-update
  9.4 1.4 multiply_reduce_fusion.1
  10.8 0.9 multiply_convert_fusion
  11.7 6.0 %collective-permute-start = (bf16[2,128,1536]{2,1,0:T(8,128)(2,1)S(1)}, bf16[2,128,1536]{2,1,0:T(8,128)(2,1)S(1)}, u32[]{:S(2)}, u32[]{:S(2)}) collective-permute-start(bf16[2,128,1536]{2,1,0:T(8,128)(2,1)S(1)} %multiply_convert_fusion), channel_id=1, source_target_pairs={{0,8},{1,9},{2,10},{3,11},{4,12},{5,13},{6,14},{7,15},{16,24},{17,... | collective-permute-start | bytes 2359304 | tf_op jit(solution)/shard_map/ppermute | solution.py:12
  17.8 1.3 collective-permute-start.1
  20.6 50.1 %all-reduce = bf16[512]{0:T(512)(128)(2,1)S(1)} all-reduce(bf16[512]{0:T(512)(128)(2,1)S(1)} %dynamic-update-slice), channel_id=1, replica_groups=mesh['grp'=2,'seq'=16] {'seq'}, use_global_device_ids=true, to_apply=%add | all-reduce | flops 512 | bytes 2048
  70.7 31.3 %all-gather.4.cloned.1.call-done = bf16[3,1536,768]{2,1,0:T(8,128)(2,1)} async-done(((bf16[3,96,768]{2,1,0:T(8,128)(2,1)}), bf16[3,1536,768]{2,1,0:T(8,128)(2,1)}) %all-gather.4.cloned.1.call-update) | async-done | bytes 7077904 | tf_op jit(solution)/shard_map/all_gather | solution.py:45
  101.9 2.4 fusion.2
  104.4 2.4 fusion.8
  106.8 2.5 fusion.7
  109.4 33.0 %all-gather.8.cloned.1.call-done = bf16[1536,512]{0,1:T(8,128)(2,1)} async-done(((bf16[1536,32]{0,1:T(8,128)(2,1)}), bf16[1536,512]{0,1:T(8,128)(2,1)}) %all-gather.8.cloned.1.call-update) | async-done | bytes 1572880 | tf_op jit(solution)/shard_map/all_gather | solution.py:64
  142.3 43.3 %all-gather.6.cloned.1.call-done = bf16[768,1536]{0,1:T(8,128)(2,1)} async-done(((bf16[768,96]{0,1:T(8,128)(2,1)}), bf16[768,1536]{0,1:T(8,128)(2,1)}) %all-gather.6.cloned.1.call-update) | async-done | bytes 2359312 | tf_op jit(solution)/shard_map/all_gather | solution.py:46
  185.7 4.6 %fusion.25 = (f32[]{:T(128)}, bf16[256,512]{1,0:T(8,128)(2,1)S(1)}) fusion(s32[2,128,512]{2,1,0:T(8,128)S(1)} %copy-done.3, f32[512]{0:T(512)S(1)} %add.86, bf16[1536,512]{0,1:T(8,128)(2,1)} %all-gather.8.cloned.1.call-done, bf16[768,1536]{0,1:T(8,128)(2,1)} %all-gather.6.cloned.1.call-done, f32[256,768]{1,0:T(8,128)S(1)} %fusion.7, ...), kind=kOutput, calls=%fused_computation.40 | convolution fusion | flops 1012072448 | bytes 6293508 | tf_op jit(solution)/shard_map/dot_general | solution.py:21
  190.2 2.1 fusion.44
  192.6 1.1 fusion.15
  193.6 1.3 collective-permute-start.2
  194.9 5.5 %collective-permute-start.3 = (bf16[2,128,768]{2,1,0:T(8,128)(2,1)S(1)}, bf16[2,128,768]{2,1,0:T(8,128)(2,1)S(1)}, u32[]{:S(2)}, u32[]{:S(2)}) collective-permute-start(bf16[2,128,768]{2,1,0:T(8,128)(2,1)S(1)} %bitcast.63), channel_id=1, source_target_pairs={{0,8},{1,9},{2,10},{3,11},{4,12},{5,13},{6,14},{7,15},{16,24},{17,... | collective-permute-start | bytes 1179656 | tf_op jit(solution)/shard_map/ppermute | solution.py:12
  200.4 3.7 %fusion.1 = f32[256,1536]{1,0:T(8,128)} fusion(bf16[256,768]{1,0:T(8,128)(2,1)S(1)} %fusion.15, bf16[3,1536,768]{2,1,0:T(8,128)(2,1)} %all-gather.4.cloned.1.call-done), kind=kOutput, calls=%fused_computation.8 | convolution fusion | flops 603979776 | bytes 4325376 | tf_op jit(solution)/shard_map/dot_general | solution.py:35
  204.1 32.7 %psum.7 = f32[]{:T(128)} all-reduce(f32[]{:T(128)} %get-tuple-element.2), channel_id=1, replica_groups=mesh['grp'=2,'seq'=16] {'seq'}, use_global_device_ids=true, to_apply=%region_3.4 | all-reduce | flops 1 | bytes 8 | tf_op jit(solution)/shard_map/psum | solution.py:68
  237.5 2.9 %convolution_add_fusion.1 = f32[256,1536]{1,0:T(8,128)S(1)} fusion(f32[256,1536]{1,0:T(8,128)} %fusion.1, bf16[256,768]{1,0:T(8,128)(2,1)S(1)} %bitcast.59, bf16[3,1536,768]{2,1,0:T(8,128)(2,1)} %all-gather.4.cloned.1.call-done), kind=kOutput, calls=%fused_computation.1 | convolution fusion | flops 604372992 | bytes 5898240 | tf_op jit(solution)/shard_map/dot_general | solution.py:35
  240.4 2.5 convolution_add_fusion
  243.3 1.3 fusion.6
  (30 shorter events, 1.5 us)
Async XLA Ops:
  7.2 11.9 %copy-start.5 = (u32[32]{0:T(128)S(1)}, u32[32]{0:T(128)}, u32[]{:S(2)}) copy-start(u32[32]{0:T(128)} %constant.32) | copy-start | bytes 388
  7.2 3.6 %copy-start = (bf16[2,128,1536]{2,1,0:T(8,128)(2,1)S(1)}, bf16[2,128,1536]{2,1,0:T(8,128)(2,1)}, u32[]{:S(2)}) copy-start(bf16[2,128,1536]{2,1,0:T(8,128)(2,1)} %param.7) | copy-start | bytes 2359300
  7.2 13.2 %copy-start.4 = (bf16[1,32]{1,0:T(2,128)(2,1)S(1)}, bf16[1,32]{1,0:T(2,128)(2,1)}, u32[]{:S(2)}) copy-start(bf16[1,32]{1,0:T(2,128)(2,1)} %param.12) | copy-start | bytes 196
  7.2 94.7 %all-gather.4.cloned.1.call-start = ((), (), s32[]{:S(2)}) async-start(), calls=%async_computation | async-start | bytes 7520256 | tf_op jit(solution)/shard_map/all_gather | solution.py:45
  7.9 134.4 %all-gather.8.cloned.1.call-start = ((), (), s32[]{:S(2)}) async-start(), calls=%async_computation.2 | async-start | bytes 1671168 | tf_op jit(solution)/shard_map/all_gather | solution.py:64
  8.7 177.0 %all-gather.6.cloned.1.call-start = ((), (), s32[]{:S(2)}) async-start(), calls=%async_computation.1 | async-start | bytes 2506752 | tf_op jit(solution)/shard_map/all_gather | solution.py:46
  11.7 92.6 %collective-permute-start = (bf16[2,128,1536]{2,1,0:T(8,128)(2,1)S(1)}, bf16[2,128,1536]{2,1,0:T(8,128)(2,1)S(1)}, u32[]{:S(2)}, u32[]{:S(2)}) collective-permute-start(bf16[2,128,1536]{2,1,0:T(8,128)(2,1)S(1)} %multiply_convert_fusion), channel_id=1, source_target_pairs={{0,8},{1,9},{2,10},{3,11},{4,12},{5,13},{6,14},{7,15},{16,24},{17,... | collective-permute-start | bytes 2359304 | tf_op jit(solution)/shard_map/ppermute | solution.py:12
  17.8 89.1 %collective-permute-start.1 = (bf16[2,128,1536]{2,1,0:T(8,128)(2,1)S(1)}, bf16[2,128,1536]{2,1,0:T(8,128)(2,1)S(1)}, u32[]{:S(2)}, u32[]{:S(2)}) collective-permute-start(bf16[2,128,1536]{2,1,0:T(8,128)(2,1)S(1)} %multiply_convert_fusion), channel_id=1, source_target_pairs={{8,0},{9,1},{10,2},{11,3},{12,4},{13,5},{14,6},{15,7},{24,16},{25,... | collective-permute-start | bytes 2359304 | tf_op jit(solution)/shard_map/ppermute | solution.py:12
  106.8 78.8 %copy-start.3 = (s32[2,128,512]{2,1,0:T(8,128)S(1)}, s32[2,128,512]{2,1,0:T(8,128)}, u32[]{:S(2)}) copy-start(s32[2,128,512]{2,1,0:T(8,128)} %param.13) | copy-start | bytes 1572868
  109.4 80.9 %copy-start.6 = (f32[256,768]{1,0:T(8,128)}, f32[256,768]{1,0:T(8,128)S(1)}, u32[]{:S(2)}) copy-start(f32[256,768]{1,0:T(8,128)S(1)} %fusion.7) | copy-start | bytes 2359300
  190.2 2.1 copy-start.2
  190.2 2.3 copy-start.7
  193.6 43.8 %collective-permute-start.2 = (bf16[2,128,768]{2,1,0:T(8,128)(2,1)S(1)}, bf16[2,128,768]{2,1,0:T(8,128)(2,1)S(1)}, u32[]{:S(2)}, u32[]{:S(2)}) collective-permute-start(bf16[2,128,768]{2,1,0:T(8,128)(2,1)S(1)} %bitcast.62), channel_id=1, source_target_pairs={{8,0},{9,1},{10,2},{11,3},{12,4},{13,5},{14,6},{15,7},{24,16},{25,... | collective-permute-start | bytes 1179656 | tf_op jit(solution)/shard_map/ppermute | solution.py:12
  194.9 45.5 %collective-permute-start.3 = (bf16[2,128,768]{2,1,0:T(8,128)(2,1)S(1)}, bf16[2,128,768]{2,1,0:T(8,128)(2,1)S(1)}, u32[]{:S(2)}, u32[]{:S(2)}) collective-permute-start(bf16[2,128,768]{2,1,0:T(8,128)(2,1)S(1)} %bitcast.63), channel_id=1, source_target_pairs={{0,8},{1,9},{2,10},{3,11},{4,12},{5,13},{6,14},{7,15},{16,24},{17,... | collective-permute-start | bytes 1179656 | tf_op jit(solution)/shard_map/ppermute | solution.py:12
  240.4 2.5 %copy-start.1 = (f32[1536]{0:T(1024)S(1)}, f32[1536]{0:T(1024)}, u32[]{:S(2)}) copy-start(f32[1536]{0:T(1024)} %param.8) | copy-start | bytes 18436
Sparse Core Ops, SparseCore 0:
  10.3 91.5 all-gather.3
  104.2 38.0 all-gather.7
  144.6 41.0 all-gather.5
where the time goes:
time: 253 us; the launch traced here: 252 us
  waiting for transfers between devices  110 us (43%)
  blocking collectives  82.7 us (33%)
  matrix products  24.3 us (10%)
  between operations  16.4 us (6%)
  starting transfers between devices  14.2 us (6%)
  other arithmetic  4.01 us (2%)
    unnamed x1, blocking collectives  50.1 us
    all_gather x1, waiting for transfers between devices, shards(): lax.all_gather(proj_weight, 'seq', axis=1, tiled=True)  43.3 us
    all_gather x1, waiting for transfers between devices, shards(): lax.all_gather(head_weight, 'seq', axis=1, tiled=True)  33 us
    psum x1, blocking collectives, shards(): summed_loss = lax.psum(loss_total, 'seq')  32.7 us
    all_gather x1, waiting for transfers between devices, shards(): lax.all_gather(conv_weight, 'seq', axis=1, tiled=True)  31.3 us
    ppermute x4, starting transfers between devices, shifted(): lax.ppermute(value, axis, [(source, source + steps) for source in range(i...  14.1 us
    dot_general x4, matrix products, back_dot(): lax.dot_general(left, right, (((1,), (1,)), ((), ())), preferred_element_...  10.2 us
  transfers between devices with their start and end apart: 7, of which 3 were waited for; matrix products, arithmetic and copies ran while one was open for 7% of the time, Pallas kernels for 0%

commit v1 on v0

--- a/solution.py
+++ b/solution.py
@@ -1,9 +1,18 @@
+import functools
+
 import jax
+import jax.experimental.pallas as pl
+import jax.experimental.pallas.tpu as pltpu
 import jax.numpy as jnp
 from jax import lax
 from jax.sharding import PartitionSpec as P
 
 SPAN = 8
+MESH = pl.DeviceIdType.MESH
+LANES = 128
+EPS = 1e-06
+GELU_K = 0.7978845608028654
+GELU_C = 0.044715
 
 
 def shifted(value, axis, steps):
@@ -84,6 +93,320 @@
     return (input_grad, loss_value)
 
 
+def dot_nn(left, right):
+    return jnp.dot(left, right, preferred_element_type=jnp.float32)
+
+
+def block_kernel(
+    n, bins_total, x_ref, gain_ref, conv_ref, proj_ref, head_ref, counts_ref, out_ref, loss_ref,
+    convf, projf, headf, normed, q_out, q_in, pre, act, stream, res, pg, pg_in, ng, losses,
+    z_send, z_recv, x_send, x_recv, c_send, c_recv, q_send, q_recv, g_send, g_recv, l_send, l_recv,
+):
+    me = lax.axis_index("seq")
+    nz = n // 4
+    core = me % 2
+    col = (me // 2) % 2
+    z = me // 4
+    low = z // (nz // 2)
+    tap = 2 * low
+    partner = (me + n // 2) % n
+    x_peer = z * 4 + (1 - col) * 2 + core
+    c_peer = z * 4 + col * 2 + (1 - core)
+    rows, width = x_ref.shape
+    inner = convf.shape[2]
+    depths = (conv_ref.shape[1], proj_ref.shape[0], head_ref.shape[0])
+    shards_in = (conv_ref, proj_ref, head_ref)
+    fulls = (convf, projf, headf)
+
+    def place(u, zs, xs, cs, part):
+        depth = depths[u]
+        start = pl.multiple_of((zs * 4 + xs * 2 + cs) * depth, depth)
+        if u == 0:
+            taps = pl.ds(low, 2) if part else slice(None)
+            return convf.at[taps, pl.ds(start, depth), :]
+        return fulls[u].at[pl.ds(start, depth), :]
+
+    def mine(u, part):
+        if u == 0 and part:
+            return conv_ref.at[pl.ds(low, 2)]
+        return shards_in[u]
+
+    def remote(src, dst, send, recv, target):
+        return pltpu.make_async_remote_copy(
+            src_ref=src, dst_ref=dst, send_sem=send, recv_sem=recv,
+            device_id={"seq": target}, device_id_type=MESH,
+        )
+
+    def z_copy(u, zs, way, own=False):
+        dst = place(u, zs, col, core, False)
+        src = mine(u, False) if own else dst
+        return remote(src, dst, z_send.at[u, zs, way], z_recv.at[u, zs], me + (4 if way == 0 else -4))
+
+    def x_copy(u, zs, own=False):
+        dst = place(u, zs, col, core, True)
+        src = mine(u, True) if own else dst
+        return remote(src, dst, x_send.at[u, zs], x_recv.at[u, zs], x_peer)
+
+    def c_copy(u, zs, xs, own=False):
+        dst = place(u, zs, xs, core, True)
+        src = mine(u, True) if own else dst
+        return remote(src, dst, c_send.at[u, zs, xs], c_recv.at[u, zs, xs], c_peer)
+
+    def own_sends(u):
+        @pl.when(z < nz - 1)
+        def _():
+            z_copy(u, z, 0, True).start()
+
+        @pl.when(z > 0)
+        def _():
+            z_copy(u, z, 1, True).start()
+
+        x_copy(u, z, True).start()
+        c_copy(u, z, col, True).start()
+
+    def z_events(u):
+        for step in range(1, nz):
+            @pl.when(z - step >= 0)
+            def _():
+                zs = z - step
+                z_copy(u, zs, 0).wait_recv()
+
+                @pl.when(z < nz - 1)
+                def _():
+                    z_copy(u, zs, 0).start()
+
+                x_copy(u, zs).start()
+                c_copy(u, zs, col).start()
+
+            @pl.when(z + step < nz)
+            def _():
+                zs = z + step
+                z_copy(u, zs, 1).wait_recv()
+
+                @pl.when(z > 0)
+                def _():
+                    z_copy(u, zs, 1).start()
+
+                x_copy(u, zs).start()
+                c_copy(u, zs, col).start()
+
+    def arrived(u, zs, xs, cs, sem):
+        dst = place(u, zs, xs, cs, True)
+        return remote(dst, dst, sem, sem, me)
+
+    def x_events(u):
+        for step in range(nz):
+            zs = (z + step) % nz
+            pltpu.make_async_remote_copy(
+                src_ref=place(u, zs, 1 - col, core, True), dst_ref=place(u, zs, 1 - col, core, True),
+                send_sem=x_send.at[u, zs], recv_sem=x_recv.at[u, zs],
+                device_id={"seq": x_peer}, device_id_type=MESH,
+            ).wait_recv()
+            c_copy(u, zs, 1 - col).start()
+
+    def c_waits(u):
+        for xs in range(2):
+            for zs in range(nz):
+                dst = place(u, zs, xs, 1 - core, True)
+                remote(dst, dst, c_send.at[u, zs, xs], c_recv.at[u, zs, xs], c_peer).wait_recv()
+
+    barrier = pltpu.get_barrier_semaphore()
+    for off in range(1, n):
+        pl.semaphore_signal(barrier, inc=1, device_id={"seq": (me + off) % n}, device_id_type=MESH)
+    pl.semaphore_wait(barrier, n - 1)
+
+    own_sends(0)
+    for u in range(3):
+        depth = depths[u]
+        start = pl.multiple_of(me * depth, depth)
+        if u == 0:
+            convf[:, pl.ds(start, depth), :] = conv_ref[...]
+        else:
+            fulls[u][pl.ds(start, depth), :] = shards_in[u][...]
+    xf = x_ref[...].astype(jnp.float32)
+    scale = lax.rsqrt(jnp.mean(xf * xf, axis=-1, keepdims=True) + EPS)
+    normed[...] = (xf * scale * gain_ref[...]).astype(jnp.bfloat16)
+    z_events(0)
+    own_sends(1)
+    own_sends(2)
+    x_events(0)
+    c_waits(0)
+
+    chunks = q_out.shape[0]
+    wide = inner // chunks
+
+    def q_copy(k):
+        return remote(q_out.at[k], q_in.at[k], q_send.at[k], q_recv.at[k], partner)
+
+    def g_copy(k):
+        return remote(pg.at[k], pg_in.at[k], g_send.at[k], g_recv.at[k], partner)
+
+    for k in range(chunks):
+        cols = slice(k * wide, (k + 1) * wide)
+        q_out[k] = dot_nn(normed[...], convf[tap, :, cols]).astype(jnp.bfloat16)
+        q_copy(k).start()
+    z_events(1)
+    z_events(2)
+    for k in range(chunks):
+        cols = slice(k * wide, (k + 1) * wide)
+        pre[:, cols] = dot_nn(normed[...], convf[1, :, cols])
+    x_events(1)
+    x_events(2)
+    for k in range(chunks):
+        cols = slice(k * wide, (k + 1) * wide)
+        q_copy(k).wait_recv()
+        v = pre[:, cols] + q_in[k].astype(jnp.float32)
+        pre[:, cols] = v
+        act[:, cols] = (0.5 * v * (1.0 + jnp.tanh(GELU_K * (v + GELU_C * v * v * v)))).astype(jnp.bfloat16)
+    c_waits(1)
+    for k in range(width // 512):
+        cols = slice(k * 512, (k + 1) * 512)
+        stream[:, cols] = (
+            x_ref[:, cols].astype(jnp.float32) + back_dot(act[...], projf[cols, :])
+        ).astype(jnp.bfloat16)
+    lane = lax.broadcasted_iota(jnp.int32, (rows, LANES), 1)
+    stream[:, width:] = jnp.where(lane == 0, 1.0, 0.0).astype(jnp.bfloat16)
+    c_waits(2)
+    logits = back_dot(stream[...], headf[...])
+    expo = jnp.exp(-jnp.abs(logits))
+    rate = jnp.maximum(logits, 0.0) + jnp.log1p(expo) + 0.05
+    seen = counts_ref[...].astype(jnp.float32)
+    terms = rate - seen * jnp.log(rate)
+    losses[me] = jnp.broadcast_to(jnp.sum(terms), losses.shape[1:])
+    inv = 1.0 / (1.0 + expo)
+    sig = jnp.where(logits >= 0, inv, expo * inv)
+    lg = ((1.0 - seen / rate) * sig).astype(jnp.bfloat16)
+
+    def l_copy(off):
+        return remote(losses.at[me], losses.at[me], l_send.at[off], l_recv.at[me], (me + off) % n)
+
+    for off in range(1, n):
+        l_copy(off).start()
+    for k in range(width // 512):
+        cols = slice(k * 512, (k + 1) * 512)
+        part = dot_nn(lg, headf[:, cols])
+        res[:, cols] = part
+        normed[:, cols] = part.astype(jnp.bfloat16)
+    for k in range(chunks):
+        cols = slice(k * wide, (k + 1) * wide)
+        ag = dot_nn(normed[...], projf[:, cols])
+        v = pre[:, cols]
+        th = jnp.tanh(GELU_K * (v + GELU_C * v * v * v))
+        slope = 0.5 * (1.0 + th) + 0.5 * v * (1.0 - th * th) * (GELU_K * (1.0 + 3.0 * GELU_C * v * v))
+        pg[k] = (ag * slope).astype(jnp.bfloat16)
+        g_copy(k).start()
+    for k in range(width // 512):
+        cols = slice(k * 512, (k + 1) * 512)
+        total = back_dot(pg[0], convf[1, cols, :wide])
+        for j in range(1, chunks):
+            total = total + back_dot(pg[j], convf[1, cols, j * wide:(j + 1) * wide])
+        ng[:, cols] = total
+    for j in range(chunks):
+        g_copy(j).wait_recv()
+        for k in range(width // 512):
+            cols = slice(k * 512, (k + 1) * 512)
+            ng[:, cols] += back_dot(pg_in[j], convf[tap, cols, j * wide:(j + 1) * wide])
+    xf = x_ref[...].astype(jnp.float32)
+    scale = lax.rsqrt(jnp.mean(xf * xf, axis=-1, keepdims=True) + EPS)
+    dy = ng[...] * gain_ref[...]
+    inner_mean = jnp.mean(xf * dy, axis=-1, keepdims=True)
+    out_ref[...] = (res[...] + (scale * dy - xf * (scale * scale * scale * inner_mean))).astype(jnp.bfloat16)
+
+    for off in range(1, n):
+        source = (me + off) % n
+        remote(losses.at[source], losses.at[source], l_send.at[off], l_recv.at[source], source).wait_recv()
+    total = losses[0]
+    for k in range(1, n):
+        total = total + losses[k]
+    loss_ref[...] = total * (1.0 / bins_total)
+
+    for off in range(1, n):
+        l_copy(off).wait_send()
+    for k in range(chunks):
+        q_copy(k).wait_send()
+        g_copy(k).wait_send()
+    for u in range(3):
+        for zs in range(nz):
+            up = (z < nz - 1) & (zs <= z)
+            down = (z > 0) & (zs >= z)
+
+            @pl.when(up)
+            def _():
+                z_copy(u, zs, 0).wait_send()
+
+            @pl.when(down)
+            def _():
+                z_copy(u, zs, 1).wait_send()
+
+            x_copy(u, zs).wait_send()
+            for xs in range(2):
+                c_copy(u, zs, xs).wait_send()
+
+
+def paired(inputs, gain, conv_weight, proj_weight, head_weight, track_head_bias, counts):
+    n = lax.axis_size("seq")
+    seq_count, row_count, width = inputs.shape
+    rows = seq_count * row_count
+    tracks = counts.shape[2]
+    inner = conv_weight.shape[2]
+    nz = n // 4
+    chunks = 3 if inner % (3 * LANES) == 0 else 1
+    head_t = jnp.concatenate(
+        [head_weight.T, jnp.pad(track_head_bias.T, ((0, 0), (0, LANES - 1)))], axis=1
+    )
+    vmem = pl.BlockSpec(memory_space=pltpu.VMEM)
+    bf, f32 = jnp.bfloat16, jnp.float32
+    dma = pltpu.SemaphoreType.DMA
+    out, loss = pl.pallas_call(
+        functools.partial(block_kernel, n, rows * n * tracks),
+        out_shape=(
+            jax.ShapeDtypeStruct((rows, width), bf),
+            jax.ShapeDtypeStruct((8, LANES), f32),
+        ),
+        in_specs=[vmem] * 6,
+        out_specs=(vmem, vmem),
+        scratch_shapes=[
+            pltpu.VMEM((3, conv_weight.shape[1] * n, inner), bf),
+            pltpu.VMEM((width, inner), bf),
+            pltpu.VMEM((tracks, width + LANES), bf),
+            pltpu.VMEM((rows, width), bf),
+            pltpu.VMEM((chunks, rows, inner // chunks), bf),
+            pltpu.VMEM((chunks, rows, inner // chunks), bf),
+            pltpu.VMEM((rows, inner), f32),
+            pltpu.VMEM((rows, inner), bf),
+            pltpu.VMEM((rows, width + LANES), bf),
+            pltpu.VMEM((rows, width), f32),
+            pltpu.VMEM((chunks, rows, inner // chunks), bf),
+            pltpu.VMEM((chunks, rows, inner // chunks), bf),
+            pltpu.VMEM((rows, width), f32),
+            pltpu.VMEM((n, 8, LANES), f32),
+            dma((3, nz, 2)), dma((3, nz)), dma((3, nz)), dma((3, nz)),
+            dma((3, nz, 2)), dma((3, nz, 2)),
+            dma((chunks,)), dma((chunks,)), dma((chunks,)), dma((chunks,)),
+            dma((n,)), dma((n,)),
+        ],
+        compiler_params=pltpu.CompilerParams(
+            collective_id=0, has_side_effects=True, vmem_limit_bytes=58 * 1024 * 1024
+        ),
+    )(
+        inputs.reshape(rows, width), gain.reshape(1, width), conv_weight, proj_weight.T,
+        head_t, counts.reshape(rows, tracks),
+    )
+    return out.reshape(inputs.shape), loss[0, :1]
+
+
+def fits(mesh, conv_weight, proj_weight, head_weight, inputs):
+    n = mesh.shape["seq"]
+    shard = conv_weight.shape[1] // n
+    return (
+        n == 2 * SPAN
+        and shard % 16 == 0
+        and (head_weight.shape[1] // n) % 16 == 0
+        and inputs.shape[2] % 512 == 0
+        and head_weight.shape[1] <= 1024
+    )
+
+
 def solution(mesh):
     placed = (
         P("grp", "seq", None),
@@ -94,10 +417,15 @@
         P(None, "seq"),
         P("grp", "seq", None),
     )
-    return jax.shard_map(
-        shards,
-        mesh=mesh,
-        in_specs=placed,
-        out_specs=(P("grp", "seq", None), P("grp")),
-        check_vma=False,
-    )
+
+    def run(inputs, gain, conv_weight, proj_weight, head_weight, track_head_bias, counts):
+        whole = fits(mesh, conv_weight, proj_weight, head_weight, inputs)
+        return jax.shard_map(
+            paired if whole else shards,
+            mesh=mesh,
+            in_specs=placed,
+            out_specs=(P("grp", "seq", None), P("grp")),
+            check_vma=False,
+        )(inputs, gain, conv_weight, proj_weight, head_weight, track_head_bias, counts)
+
+    return run

time: 253 us -> 109 us (0.43)
  waiting for transfers between devices: 110 us -> 0 us
  Pallas kernels: 0 us -> 101 us
  blocking collectives: 82.7 us -> 0 us
  matrix products: 24.3 us -> 0 us
  between operations: 16.4 us -> 0.65 us
  starting transfers between devices: 14.2 us -> 0 us
  local copies, waits for them, and re-layouts: 1.05 us -> 4.7 us
    all_gather x3 -> x0, waiting for transfers between devices: 108 us -> none  [the longest x1 43.3 us: shards(): lax.all_gather(proj_weight, 'seq', axis=1, tiled=True)]
    pallas_call x0 -> x1, Pallas kernels: none -> 101 us  [paired(): pl.pallas_call(functools.partial(block_kernel, n, rows * n * tracks), out...]
    unnamed x1 -> x0, blocking collectives: 50.1 us -> none
    psum x1 -> x0, blocking collectives: 32.7 us -> none  [shards(): summed_loss = lax.psum(loss_total, 'seq')]
    dot_general x9 -> x0, matrix products: 24.3 us -> none  [the longest x4 10.2 us: back_dot(): lax.dot_general(left, right, (((1,), (1,)), ((), ())), preferred_element_...]
    ppermute x4 -> x0, starting transfers between devices: 14.1 us -> none  [shifted(): lax.ppermute(value, axis, [(source, source + steps) for source in range(i...]
  transfers between devices with their start and end apart: 7 -> 0, of which waited for: 3 -> 0; matrix products, arithmetic and copies ran while one was open for 7% -> 0% of each run, Pallas kernels for 0% -> 0%
where the time goes in v1:
time: 109 us; the launch traced here: 108 us
  Pallas kernels  101 us (93%)
  local copies, waits for them, and re-layouts  4.7 us (4%)
  other arithmetic  1.55 us (1%)
    pallas_call x1, Pallas kernels, paired(): pl.pallas_call(functools.partial(block_kernel, n, rows * n * tracks), out...  101 us
    unnamed x5, local copies, waits for them, and re-layouts  2.82 us

profile of v1, /device:TPU:0, one launch (start us, length us, event | category | flops | bytes accessed | tf_op | source)
XLA Modules:
  0.0 108.2 jit_solution(12087208616980897137)
XLA Ops:
  0.6 0.0 copy-start
  0.6 0.7 copy-done
  1.3 0.0 copy-start.1
  1.3 0.6 reshape.17.gain_ref
  1.9 0.1 copy-done.1
  2.0 0.1 copy.9
  2.1 1.5 %fusion.1.head_ref = bf16[32,1664]{1,0:T(8,128)(2,1)} fusion(bf16[32,1]{1,0:T(8,128)(2,1)S(1)} %copy.9, bf16[32,1536]{1,0:T(8,128)(2,1)} %bitcast.11), kind=kLoop, calls=%fused_computation.2 | loop fusion | flops 319488 | bytes 204864 | tf_op jit(solution)/shard_map/concatenate | solution.py:354
  3.6 101.3 %shard_map.86 = (bf16[256,1536]{1,0:T(8,128)(2,1)}, f32[8,128]{1,0:T(8,128)}) custom-call(bf16[256,1536]{1,0:T(8,128)(2,1)} %bitcast.7, f32[1,1536]{1,0:T(1,128)} %reshape.17.gain_ref, bf16[3,96,768]{2,1,0:T(8,128)(2,1)} %conv_ref.1, bf16[96,768]{1,0:T(8,128)(2,1)} %bitcast.10, bf16[32,1664]{1,0:T(8,128)(2,1)} %fusion.1.head_ref, s32[256,512]{1,0:T(8,128)} %bitcast.9), custom_call_target="tpu_custom_call" | custom-call | tf_op jit(solution)/shard_map/pallas_call | solution.py:360
  105.0 1.2 %slice.3 = f32[1,1]{1,0:T(1,128)} slice(f32[8,128]{1,0:T(8,128)} %get-tuple-element.5), slice={[0:1], [0:1]} | slice | bytes 8 | tf_op jit(solution)/shard_map/slice | solution.py:395
  106.1 2.1 %copy.11 = bf16[2,128,1536]{2,1,0:T(8,128)(2,1)} copy(bf16[2,128,1536]{2,1,0:T(8,128)(2,1)} %bitcast.8) | data formatting | bytes 1572864
Async XLA Ops:
  0.6 0.7 copy-start
  1.3 0.7 copy-start.1

commit v2 on v1

--- a/solution.py
+++ b/solution.py
@@ -98,38 +98,46 @@
 
 
 def block_kernel(
-    n, bins_total, x_ref, gain_ref, conv_ref, proj_ref, head_ref, counts_ref, out_ref, loss_ref,
-    convf, projf, headf, normed, q_out, q_in, pre, act, stream, res, pg, pg_in, ng, losses,
-    z_send, z_recv, x_send, x_recv, c_send, c_recv, q_send, q_recv, g_send, g_recv, l_send, l_recv,
+    n, bins_total, x_ref, gain_ref, conv_ref, proj_ref, head_ref, bias_ref, counts_ref, out_ref, loss_ref,
+    convf, projf, headf, head_own, normed, q_out, q_in, pre, act, stream, res, pg, pg_in, ng, losses,
+    z_send, z_recv, x_send, x_recv, y_send, y_recv, c_send, c_recv,
+    q_send, q_recv, g_send, g_recv, l_send, l_recv, own_sem,
 ):
     me = lax.axis_index("seq")
+    grp = lax.axis_index("grp")
     nz = n // 4
+    half = nz // 2
     core = me % 2
     col = (me // 2) % 2
     z = me // 4
-    low = z // (nz // 2)
+    low = z // half
     tap = 2 * low
     partner = (me + n // 2) % n
     x_peer = z * 4 + (1 - col) * 2 + core
     c_peer = z * 4 + col * 2 + (1 - core)
     rows, width = x_ref.shape
     inner = convf.shape[2]
-    depths = (conv_ref.shape[1], proj_ref.shape[0], head_ref.shape[0])
-    shards_in = (conv_ref, proj_ref, head_ref)
-    fulls = (convf, projf, headf)
-
-    def place(u, zs, xs, cs, part):
-        depth = depths[u]
-        start = pl.multiple_of((zs * 4 + xs * 2 + cs) * depth, depth)
-        if u == 0:
-            taps = pl.ds(low, 2) if part else slice(None)
-            return convf.at[taps, pl.ds(start, depth), :]
-        return fulls[u].at[pl.ds(start, depth), :]
-
-    def mine(u, part):
-        if u == 0 and part:
-            return conv_ref.at[pl.ds(low, 2)]
-        return shards_in[u]
+    conv_depth = conv_ref.shape[1]
+    depths = (conv_depth, conv_depth, proj_ref.shape[0], head_ref.shape[0], conv_depth)
+    taps = (tap, 1, None, None, 2 - tap)
+    slots = (4 * low, 1, 2, 3, 4 * (1 - low))
+    can_up = ((z < nz - 1) & (z != half - 1), z < nz - 1, z < nz - 1, z < nz - 1, low == 0)
+    can_down = ((z > 0) & (z != half), z > 0, z > 0, z > 0, low == 1)
+
+    def place(u, zs, xs, cs):
+        start = pl.multiple_of((zs * 4 + xs * 2 + cs) * depths[u], depths[u])
+        if u == 2:
+            return projf.at[pl.ds(start, depths[u]), :]
+        if u == 3:
+            return headf.at[pl.ds(start, depths[u]), :]
+        return convf.at[taps[u], pl.ds(start, depths[u]), :]
+
+    def mine(u):
+        if u == 2:
+            return proj_ref
+        if u == 3:
+            return head_own
+        return conv_ref.at[taps[u]]
 
     def remote(src, dst, send, recv, target):
         return pltpu.make_async_remote_copy(
@@ -138,98 +146,127 @@
         )
 
     def z_copy(u, zs, way, own=False):
-        dst = place(u, zs, col, core, False)
-        src = mine(u, False) if own else dst
-        return remote(src, dst, z_send.at[u, zs, way], z_recv.at[u, zs], me + (4 if way == 0 else -4))
+        dst = place(u, zs, col, core)
+        src = mine(u) if own else dst
+        target = me + (4 if way == 0 else -4)
+        return remote(src, dst, z_send.at[slots[u], zs, way], z_recv.at[slots[u], zs], target)
 
     def x_copy(u, zs, own=False):
-        dst = place(u, zs, col, core, True)
-        src = mine(u, True) if own else dst
+        dst = place(u, zs, col, core)
+        src = mine(u) if own else dst
         return remote(src, dst, x_send.at[u, zs], x_recv.at[u, zs], x_peer)
 
+    def y_copy(u, zs):
+        dst = place(u, zs, 1 - col, core)
+        return pltpu.make_async_remote_copy(
+            src_ref=dst, dst_ref=dst, send_sem=y_send.at[u, zs], recv_sem=y_recv.at[u, zs],
+            device_id={"grp": 1 - grp}, device_id_type=MESH,
+        )
+
     def c_copy(u, zs, xs, own=False):
-        dst = place(u, zs, xs, core, True)
-        src = mine(u, True) if own else dst
+        dst = place(u, zs, xs, core)
+        src = mine(u) if own else dst
         return remote(src, dst, c_send.at[u, zs, xs], c_recv.at[u, zs, xs], c_peer)
 
+    def spread(u, zs, own=False):
+        @pl.when(zs % 2 == grp)
+        def _():
+            x_copy(u, zs, own).start()
+
+        c_copy(u, zs, col, own).start()
+
     def own_sends(u):
-        @pl.when(z < nz - 1)
+        @pl.when(can_up[u])
         def _():
             z_copy(u, z, 0, True).start()
 
-        @pl.when(z > 0)
+        @pl.when(can_down[u])
         def _():
             z_copy(u, z, 1, True).start()
 
-        x_copy(u, z, True).start()
-        c_copy(u, z, col, True).start()
+        if u != 4:
+            spread(u, z, True)
 
     def z_events(u):
         for step in range(1, nz):
-            @pl.when(z - step >= 0)
+            @pl.when((z - step >= 0) if u != 4 else (z - step >= 0) & (low == 0))
             def _():
                 zs = z - step
                 z_copy(u, zs, 0).wait_recv()
 
-                @pl.when(z < nz - 1)
+                @pl.when(can_up[u])
                 def _():
                     z_copy(u, zs, 0).start()
 
-                x_copy(u, zs).start()
-                c_copy(u, zs, col).start()
-
-            @pl.when(z + step < nz)
+                if u != 4:
+                    spread(u, zs)
+
+            @pl.when((z + step < nz) if u != 4 else (z + step < nz) & (low == 1))
             def _():
                 zs = z + step
                 z_copy(u, zs, 1).wait_recv()
 
-                @pl.when(z > 0)
+                @pl.when(can_down[u])
                 def _():
                     z_copy(u, zs, 1).start()
 
-                x_copy(u, zs).start()
-                c_copy(u, zs, col).start()
-
-    def arrived(u, zs, xs, cs, sem):
-        dst = place(u, zs, xs, cs, True)
-        return remote(dst, dst, sem, sem, me)
+                if u != 4:
+                    spread(u, zs)
 
     def x_events(u):
         for step in range(nz):
-            zs = (z + step) % nz
-            pltpu.make_async_remote_copy(
-                src_ref=place(u, zs, 1 - col, core, True), dst_ref=place(u, zs, 1 - col, core, True),
-                send_sem=x_send.at[u, zs], recv_sem=x_recv.at[u, zs],
-                device_id={"seq": x_peer}, device_id_type=MESH,
-            ).wait_recv()
+            zs = 2 * ((z // 2 + step // 2) % (nz // 2)) + (z % 2 + step % 2) % 2
+            dst = place(u, zs, 1 - col, core)
+
+            @pl.when(zs % 2 == grp)
+            def _():
+                remote(dst, dst, x_send.at[u, zs], x_recv.at[u, zs], x_peer).wait_recv()
+                y_copy(u, zs).start()
+
+            @pl.when(zs % 2 != grp)
+            def _():
+                y_copy(u, zs).wait_recv()
+
             c_copy(u, zs, 1 - col).start()
 
     def c_waits(u):
         for xs in range(2):
             for zs in range(nz):
-                dst = place(u, zs, xs, 1 - core, True)
+                dst = place(u, zs, xs, 1 - core)
                 remote(dst, dst, c_send.at[u, zs, xs], c_recv.at[u, zs, xs], c_peer).wait_recv()
 
+    fill = [
+        pltpu.make_async_copy(head_ref, head_own.at[:, pl.ds(0, width)], own_sem.at[0]),
+        pltpu.make_async_copy(bias_ref, head_own.at[:, pl.ds(width, LANES)], own_sem.at[1]),
+    ]
+    for copy in fill:
+        copy.start()
     barrier = pltpu.get_barrier_semaphore()
     for off in range(1, n):
         pl.semaphore_signal(barrier, inc=1, device_id={"seq": (me + off) % n}, device_id_type=MESH)
-    pl.semaphore_wait(barrier, n - 1)
+    pl.semaphore_signal(barrier, inc=1, device_id={"grp": 1 - grp}, device_id_type=MESH)
+    pl.semaphore_wait(barrier, n)
 
     own_sends(0)
-    for u in range(3):
-        depth = depths[u]
-        start = pl.multiple_of(me * depth, depth)
-        if u == 0:
-            convf[:, pl.ds(start, depth), :] = conv_ref[...]
-        else:
-            fulls[u][pl.ds(start, depth), :] = shards_in[u][...]
+    own_sends(4)
+    own_sends(1)
+    for copy in fill:
+        copy.wait()
+    rows_of = [pl.ds(pl.multiple_of(me * depths[u], depths[u]), depths[u]) for u in range(4)]
+    convf[tap, rows_of[0], :] = conv_ref[tap]
+    convf[1, rows_of[1], :] = conv_ref[1]
+    projf[rows_of[2], :] = proj_ref[...]
+    headf[rows_of[3], :] = head_own[...]
     xf = x_ref[...].astype(jnp.float32)
     scale = lax.rsqrt(jnp.mean(xf * xf, axis=-1, keepdims=True) + EPS)
     normed[...] = (xf * scale * gain_ref[...]).astype(jnp.bfloat16)
+    z_events(4)
     z_events(0)
-    own_sends(1)
     own_sends(2)
+    own_sends(3)
+    z_events(1)
     x_events(0)
+    z_events(2)
     c_waits(0)
 
     chunks = q_out.shape[0]
@@ -245,20 +282,21 @@
         cols = slice(k * wide, (k + 1) * wide)
         q_out[k] = dot_nn(normed[...], convf[tap, :, cols]).astype(jnp.bfloat16)
         q_copy(k).start()
-    z_events(1)
-    z_events(2)
+    z_events(3)
+    x_events(1)
+    c_waits(1)
     for k in range(chunks):
         cols = slice(k * wide, (k + 1) * wide)
         pre[:, cols] = dot_nn(normed[...], convf[1, :, cols])
-    x_events(1)
     x_events(2)
+    x_events(3)
     for k in range(chunks):
         cols = slice(k * wide, (k + 1) * wide)
         q_copy(k).wait_recv()
         v = pre[:, cols] + q_in[k].astype(jnp.float32)
         pre[:, cols] = v
         act[:, cols] = (0.5 * v * (1.0 + jnp.tanh(GELU_K * (v + GELU_C * v * v * v)))).astype(jnp.bfloat16)
-    c_waits(1)
+    c_waits(2)
     for k in range(width // 512):
         cols = slice(k * 512, (k + 1) * 512)
         stream[:, cols] = (
@@ -266,7 +304,7 @@
         ).astype(jnp.bfloat16)
     lane = lax.broadcasted_iota(jnp.int32, (rows, LANES), 1)
     stream[:, width:] = jnp.where(lane == 0, 1.0, 0.0).astype(jnp.bfloat16)
-    c_waits(2)
+    c_waits(3)
     logits = back_dot(stream[...], headf[...])
     expo = jnp.exp(-jnp.abs(logits))
     rate = jnp.maximum(logits, 0.0) + jnp.log1p(expo) + 0.05
@@ -318,29 +356,31 @@
     total = losses[0]
     for k in range(1, n):
         total = total + losses[k]
-    loss_ref[...] = total * (1.0 / bins_total)
+    loss_ref[0] = total[0, 0] * (1.0 / bins_total)
 
     for off in range(1, n):
         l_copy(off).wait_send()
     for k in range(chunks):
         q_copy(k).wait_send()
         g_copy(k).wait_send()
-    for u in range(3):
+    for u in range(5):
         for zs in range(nz):
-            up = (z < nz - 1) & (zs <= z)
-            down = (z > 0) & (zs >= z)
-
-            @pl.when(up)
+            @pl.when(can_up[u] & (zs <= z))
             def _():
                 z_copy(u, zs, 0).wait_send()
 
-            @pl.when(down)
+            @pl.when(can_down[u] & (zs >= z))
             def _():
                 z_copy(u, zs, 1).wait_send()
 
-            x_copy(u, zs).wait_send()
-            for xs in range(2):
-                c_copy(u, zs, xs).wait_send()
+            if u != 4:
+                @pl.when(zs % 2 == grp)
+                def _():
+                    x_copy(u, zs).wait_send()
+                    y_copy(u, zs).wait_send()
+
+                for xs in range(2):
+                    c_copy(u, zs, xs).wait_send()
 
 
 def paired(inputs, gain, conv_weight, proj_weight, head_weight, track_head_bias, counts):
@@ -351,9 +391,7 @@
     inner = conv_weight.shape[2]
     nz = n // 4
     chunks = 3 if inner % (3 * LANES) == 0 else 1
-    head_t = jnp.concatenate(
-        [head_weight.T, jnp.pad(track_head_bias.T, ((0, 0), (0, LANES - 1)))], axis=1
-    )
+    bias_t = jnp.pad(track_head_bias.T, ((0, 0), (0, LANES - 1)))
     vmem = pl.BlockSpec(memory_space=pltpu.VMEM)
     bf, f32 = jnp.bfloat16, jnp.float32
     dma = pltpu.SemaphoreType.DMA
@@ -361,14 +399,15 @@
         functools.partial(block_kernel, n, rows * n * tracks),
         out_shape=(
             jax.ShapeDtypeStruct((rows, width), bf),
-            jax.ShapeDtypeStruct((8, LANES), f32),
+            jax.ShapeDtypeStruct((1,), f32),
         ),
-        in_specs=[vmem] * 6,
-        out_specs=(vmem, vmem),
+        in_specs=[vmem] * 7,
+        out_specs=(vmem, pl.BlockSpec(memory_space=pltpu.SMEM)),
         scratch_shapes=[
             pltpu.VMEM((3, conv_weight.shape[1] * n, inner), bf),
             pltpu.VMEM((width, inner), bf),
             pltpu.VMEM((tracks, width + LANES), bf),
+            pltpu.VMEM((tracks // n, width + LANES), bf),
             pltpu.VMEM((rows, width), bf),
             pltpu.VMEM((chunks, rows, inner // chunks), bf),
             pltpu.VMEM((chunks, rows, inner // chunks), bf),
@@ -380,19 +419,19 @@
             pltpu.VMEM((chunks, rows, inner // chunks), bf),
             pltpu.VMEM((rows, width), f32),
             pltpu.VMEM((n, 8, LANES), f32),
-            dma((3, nz, 2)), dma((3, nz)), dma((3, nz)), dma((3, nz)),
-            dma((3, nz, 2)), dma((3, nz, 2)),
+            dma((5, nz, 2)), dma((5, nz)), dma((4, nz)), dma((4, nz)),
+            dma((4, nz)), dma((4, nz)), dma((4, nz, 2)), dma((4, nz, 2)),
             dma((chunks,)), dma((chunks,)), dma((chunks,)), dma((chunks,)),
-            dma((n,)), dma((n,)),
+            dma((n,)), dma((n,)), dma((2,)),
         ],
         compiler_params=pltpu.CompilerParams(
             collective_id=0, has_side_effects=True, vmem_limit_bytes=58 * 1024 * 1024
         ),
     )(
         inputs.reshape(rows, width), gain.reshape(1, width), conv_weight, proj_weight.T,
-        head_t, counts.reshape(rows, tracks),
-    )
-    return out.reshape(inputs.shape), loss[0, :1]
+        head_weight.T, bias_t, counts.reshape(rows, tracks),
+    )
+    return out.reshape(inputs.shape), loss
 
 
 def fits(mesh, conv_weight, proj_weight, head_weight, inputs):
@@ -400,6 +439,7 @@
     shard = conv_weight.shape[1] // n
     return (
         n == 2 * SPAN
+        and mesh.shape["grp"] == 2
         and shard % 16 == 0
         and (head_weight.shape[1] // n) % 16 == 0
         and inputs.shape[2] % 512 == 0

time: 109 us -> 154 us (1.41)
  Pallas kernels: 101 us -> 147 us
  between operations: 0.65 us -> 2.41 us
  other arithmetic: 1.55 us -> 0 us
    pallas_call x1, Pallas kernels: 101 us -> 147 us  [paired(): pl.pallas_call(functools.partial(block_kernel, n, rows * n * tracks), out...]
    concatenate x1 -> x0, other arithmetic: 1.55 us -> none  [paired(): jnp.concatenate([head_weight.T, jnp.pad(track_head_bias.T, ((0, 0), (0, L...]
where the time goes in v2:
time: 154 us; the launch traced here: 153 us
  Pallas kernels  147 us (95%)
  local copies, waits for them, and re-layouts  4.12 us (3%)
  between operations  2.41 us (2%)
    pallas_call x1, Pallas kernels, paired(): pl.pallas_call(functools.partial(block_kernel, n, rows * n * tracks), out...  147 us

profile of v2, /device:TPU:0, one launch (start us, length us, event | category | flops | bytes accessed | tf_op | source)
XLA Modules:
  0.0 153.3 jit_solution(18274474630499021994)
XLA Ops:
  0.6 0.0 copy-start
  0.6 0.7 copy-done
  1.3 0.0 copy-start.1
  1.3 0.6 reshape.17.gain_ref
  1.9 0.1 copy-done.1
  2.0 0.1 copy.9
  2.1 0.6 pad.4.bias_ref
  2.7 146.7 %shard_map.86 = (bf16[256,1536]{1,0:T(8,128)(2,1)}, f32[1]{0:T(128)}) custom-call(bf16[256,1536]{1,0:T(8,128)(2,1)} %bitcast.6, f32[1,1536]{1,0:T(1,128)} %reshape.17.gain_ref, bf16[3,96,768]{2,1,0:T(8,128)(2,1)} %conv_ref.1, bf16[96,768]{1,0:T(8,128)(2,1)} %bitcast.9, bf16[32,1536]{1,0:T(8,128)(2,1)} %bitcast.10, bf16[32,128]{1,0:T(8,128)(2,1)} %pad.4.bias_ref, ...), custom_call_target="tpu_custom_call" | custom-call | tf_op jit(solution)/shard_map/pallas_call | solution.py:398
  149.4 2.1 %copy.12 = bf16[2,128,1536]{2,1,0:T(8,128)(2,1)} copy(bf16[2,128,1536]{2,1,0:T(8,128)(2,1)} %bitcast.7) | data formatting | bytes 1572864
Async XLA Ops:
  0.6 0.7 copy-start
  1.3 0.7 copy-start.1

commit v3 on v2

--- a/solution.py
+++ b/solution.py
@@ -169,9 +169,7 @@
         return remote(src, dst, c_send.at[u, zs, xs], c_recv.at[u, zs, xs], c_peer)
 
     def spread(u, zs, own=False):
-        @pl.when(zs % 2 == grp)
-        def _():
-            x_copy(u, zs, own).start()
+        x_copy(u, zs, own).start()
 
         c_copy(u, zs, col, own).start()
 
@@ -218,15 +216,7 @@
             zs = 2 * ((z // 2 + step // 2) % (nz // 2)) + (z % 2 + step % 2) % 2
             dst = place(u, zs, 1 - col, core)
 
-            @pl.when(zs % 2 == grp)
-            def _():
-                remote(dst, dst, x_send.at[u, zs], x_recv.at[u, zs], x_peer).wait_recv()
-                y_copy(u, zs).start()
-
-            @pl.when(zs % 2 != grp)
-            def _():
-                y_copy(u, zs).wait_recv()
-
+            remote(dst, dst, x_send.at[u, zs], x_recv.at[u, zs], x_peer).wait_recv()
             c_copy(u, zs, 1 - col).start()
 
     def c_waits(u):
@@ -374,10 +364,7 @@
                 z_copy(u, zs, 1).wait_send()
 
             if u != 4:
-                @pl.when(zs % 2 == grp)
-                def _():
-                    x_copy(u, zs).wait_send()
-                    y_copy(u, zs).wait_send()
+                x_copy(u, zs).wait_send()
 
                 for xs in range(2):
                     c_copy(u, zs, xs).wait_send()

time: 154 us -> 91.3 us (0.59)
  Pallas kernels: 147 us -> 84.5 us
    pallas_call x1, Pallas kernels: 147 us -> 84.5 us  [paired(): pl.pallas_call(functools.partial(block_kernel, n, rows * n * tracks), out...]
where the time goes in v3:
time: 91.3 us; the launch traced here: 91 us
  Pallas kernels  84.5 us (93%)
  local copies, waits for them, and re-layouts  4.12 us (5%)
  between operations  2.41 us (3%)
    pallas_call x1, Pallas kernels, paired(): pl.pallas_call(functools.partial(block_kernel, n, rows * n * tracks), out...  84.5 us
    unnamed x5, local copies, waits for them, and re-layouts  2.82 us

profile of v3, /device:TPU:0, one launch (start us, length us, event | category | flops | bytes accessed | tf_op | source)
XLA Modules:
  0.0 91.0 jit_solution(6936270287626992726)
XLA Ops:
  0.6 0.0 copy-start
  0.6 0.7 copy-done
  1.3 0.0 copy-start.1
  1.3 0.6 reshape.17.gain_ref
  1.9 0.1 copy-done.1
  2.0 0.1 copy.9
  2.1 0.6 pad.4.bias_ref
  2.7 84.5 %shard_map.86 = (bf16[256,1536]{1,0:T(8,128)(2,1)}, f32[1]{0:T(128)}) custom-call(bf16[256,1536]{1,0:T(8,128)(2,1)} %bitcast.6, f32[1,1536]{1,0:T(1,128)} %reshape.17.gain_ref, bf16[3,96,768]{2,1,0:T(8,128)(2,1)} %conv_ref.1, bf16[96,768]{1,0:T(8,128)(2,1)} %bitcast.9, bf16[32,1536]{1,0:T(8,128)(2,1)} %bitcast.10, bf16[32,128]{1,0:T(8,128)(2,1)} %pad.4.bias_ref, ...), custom_call_target="tpu_custom_call" | custom-call | tf_op jit(solution)/shard_map/pallas_call | solution.py:385
  87.2 2.1 %copy.12 = bf16[2,128,1536]{2,1,0:T(8,128)(2,1)} copy(bf16[2,128,1536]{2,1,0:T(8,128)(2,1)} %bitcast.7) | data formatting | bytes 1572864
Async XLA Ops:
  0.6 0.7 copy-start
  1.3 0.7 copy-start.1

commit v4 on v3

--- a/solution.py
+++ b/solution.py
@@ -255,8 +255,9 @@
     own_sends(2)
     own_sends(3)
     z_events(1)
+    z_events(2)
+    z_events(3)
     x_events(0)
-    z_events(2)
     c_waits(0)
 
     chunks = q_out.shape[0]
@@ -272,7 +273,6 @@
         cols = slice(k * wide, (k + 1) * wide)
         q_out[k] = dot_nn(normed[...], convf[tap, :, cols]).astype(jnp.bfloat16)
         q_copy(k).start()
-    z_events(3)
     x_events(1)
     c_waits(1)
     for k in range(chunks):

time: 91.3 us -> 96.8 us (1.060)
  Pallas kernels: 84.5 us -> 90 us
    pallas_call x1, Pallas kernels: 84.5 us -> 90 us  [paired(): pl.pallas_call(functools.partial(block_kernel, n, rows * n * tracks), out...]
where the time goes in v4:
time: 96.8 us; the launch traced here: 96.5 us
  Pallas kernels  90 us (93%)
  local copies, waits for them, and re-layouts  4.12 us (4%)
  between operations  2.41 us (2%)
    pallas_call x1, Pallas kernels, paired(): pl.pallas_call(functools.partial(block_kernel, n, rows * n * tracks), out...  90 us
    unnamed x5, local copies, waits for them, and re-layouts  2.82 us

profile of v4, /device:TPU:0, one launch (start us, length us, event | category | flops | bytes accessed | tf_op | source)
XLA Modules:
  0.0 96.5 jit_solution(2499779824905636244)
XLA Ops:
  0.6 0.0 copy-start
  0.6 0.7 copy-done
  1.3 0.0 copy-start.1
  1.3 0.6 reshape.17.gain_ref
  1.9 0.1 copy-done.1
  2.0 0.1 copy.9
  2.1 0.6 pad.4.bias_ref
  2.7 90.0 %shard_map.86 = (bf16[256,1536]{1,0:T(8,128)(2,1)}, f32[1]{0:T(128)}) custom-call(bf16[256,1536]{1,0:T(8,128)(2,1)} %bitcast.6, f32[1,1536]{1,0:T(1,128)} %reshape.17.gain_ref, bf16[3,96,768]{2,1,0:T(8,128)(2,1)} %conv_ref.1, bf16[96,768]{1,0:T(8,128)(2,1)} %bitcast.9, bf16[32,1536]{1,0:T(8,128)(2,1)} %bitcast.10, bf16[32,128]{1,0:T(8,128)(2,1)} %pad.4.bias_ref, ...), custom_call_target="tpu_custom_call" | custom-call | tf_op jit(solution)/shard_map/pallas_call | solution.py:385
  92.7 2.1 %copy.12 = bf16[2,128,1536]{2,1,0:T(8,128)(2,1)} copy(bf16[2,128,1536]{2,1,0:T(8,128)(2,1)} %bitcast.7) | data formatting | bytes 1572864
Async XLA Ops:
  0.6 0.7 copy-start
  1.3 0.7 copy-start.1
